TPU v7x, 32 devices: a whole 2x2x4 slice. The times are simulated.
32 devices in a mesh: groups: 2 (over y), blk: 4 (over z), head: 2 (over x), sub: 2 (over core).
Axes of the slice: x: 2, y: 2, z: 4, core: 2. Of those that a mesh axis runs over, the one named last changes fastest.
Arguments:
- queries: bfloat16 [128, 32, 128], P(('groups', 'blk'), ('head', 'sub')), parts along dimension 0, may hold values from -16 to 16
- key_cache: bfloat16 [2, 128, 256, 128], P('head', ('groups', 'blk')), parts along dimension 1, may hold values from -8 to 8
- cached_value_slots: bfloat16 [2, 128, 256, 128], P('head', ('groups', 'blk')), parts along dimension 1, may hold values from -6 to 6
- block_counts: int32 [8], P('groups'), parts along dimension 0, may hold values from 2 to 16, as said below
- slot_blocks: int32 [128], P('groups'), parts along dimension 0, may hold values from -1 to 31, as said below
- offsets: int32 [128], P('groups'), parts along dimension 0, may hold values from 4096 to 8192
Outputs:
- attended: bfloat16 [128, 32, 128], P(('groups', 'blk'), ('head', 'sub')), parts along dimension 0
There are 2 independent parts, one for each index of `groups`. A program takes and returns all parts, laid end to end along the dimension named above; each array names one. Nothing has to cross between parts.
Inputs may be any that keep to these rules, and one draw needn't show every extreme that they name: block_counts[i] is the number of live slots of index i of blk; the counts sum to 32. `slot_blocks`: entry i * 16 + s holds a block number when s < block_counts[i] and -1 otherwise; every block number below 32 stands in exactly one live slot.
All inputs are finite; a program needn't handle non-finite values.
Results may differ from a plain program's by a relative error of at most 0.0065.
Values may be sent and summed in bfloat16 or wider, within the bound.
No kernel may reach another device: no remote copies, remote signals or barrier semaphores. Data moves between devices by JAX's collectives and lax.ppermute only.
A program may use at most 64 MiB of HBM per device.

v0:
```python
import jax
import jax.numpy as jnp
from jax import lax
from jax.sharding import PartitionSpec as P

lowest_score = -1e30


def partner_2(x, axis, bit):
    return lax.ppermute(x, axis, [(i, i ^ 1 << bit) for i in range(lax.axis_size(axis))])


def block_update(running, q_rows, row_limit, key_block, value_block, block_id):
    row_max, row_sum, row_out = running
    block_len = key_block.shape[0]
    scores = jnp.dot(q_rows, key_block.T, preferred_element_type=jnp.float32) * key_block.shape[
        1
    ] ** (-0.5)
    position = block_id * block_len + jnp.arange(block_len, dtype=jnp.int32)
    visible = position[None, :] < row_limit[:, None]
    scores = jnp.where(visible, scores, lowest_score)
    new_max = jnp.maximum(row_max, jnp.max(scores, axis=1))
    weights = jnp.where(visible, jnp.exp(scores - new_max[:, None]), 0.0)
    factor = jnp.exp(row_max - new_max)
    new_sum = row_sum * factor + jnp.sum(weights, axis=1)
    new_out = row_out * factor[:, None] + jnp.dot(
        weights.astype(jnp.bfloat16), value_block, preferred_element_type=jnp.float32
    )
    return (new_max, new_sum, new_out)


def run_slots(running, q_rows, row_limit, key_slots, value_slots, slot_ids, lower_slot, upper_slot):

    def loop_body(slot_number, carried):
        return block_update(
            carried,
            q_rows,
            row_limit,
            key_slots[slot_number],
            value_slots[slot_number],
            slot_ids[slot_number],
        )

    return lax.fori_loop(lower_slot, upper_slot, loop_body, running)


def per_device(queries, key_cache, cached_value_slots, block_counts, slot_blocks, offsets):
    tok_dev, heads_dev, head_width = queries.shape
    key_slots = key_cache[0]
    value_slots = cached_value_slots[0]
    slot_total = key_slots.shape[0]
    half_slots = slot_total // 2
    members = lax.axis_size("blk")
    member = lax.axis_index("blk")
    own_ids = lax.dynamic_slice_in_dim(slot_blocks, member * slot_total, slot_total)
    own_count = block_counts[member]
    partner = jnp.bitwise_xor(member, members // 2)
    far_keys, far_values = partner_2(
        (key_slots[half_slots:], value_slots[half_slots:]), "blk", members.bit_length() - 2
    )
    partner_ids = lax.dynamic_slice_in_dim(
        slot_blocks, partner * slot_total + half_slots, half_slots
    )
    partner_count = block_counts[partner]
    own_moved = jnp.maximum(
        0, jnp.minimum((own_count - partner_count) // 2, own_count - half_slots)
    )
    partner_moved = jnp.maximum(
        0, jnp.minimum((partner_count - own_count) // 2, partner_count - half_slots)
    )
    work_list = [
        (key_slots, value_slots, own_ids, jnp.int32(0), own_count - own_moved),
        (
            far_keys,
            far_values,
            partner_ids,
            partner_count - partner_moved - half_slots,
            partner_count - half_slots,
        ),
    ]
    total_tok = tok_dev * members
    all_queries = lax.all_gather(queries, "blk", axis=0, tiled=True)
    q_rows = all_queries.reshape(-1, head_width)
    row_limit = jnp.repeat(offsets, heads_dev)
    count_rows = q_rows.shape[0]
    running = (
        jnp.full((count_rows,), lowest_score, jnp.float32),
        jnp.zeros((count_rows,), jnp.float32),
        jnp.zeros((count_rows, head_width), jnp.float32),
    )
    for key_part, value_part, part_ids, lower_slot, upper_slot in work_list:
        running = run_slots(
            running, q_rows, row_limit, key_part, value_part, part_ids, lower_slot, upper_slot
        )
    row_max, row_sum, row_out = running
    row_max = row_max.reshape(total_tok, heads_dev)
    row_sum = row_sum.reshape(total_tok, heads_dev)
    row_out = row_out.reshape(total_tok, heads_dev, head_width)
    peer_max, peer_sum, peer_out = (
        lax.all_to_all(row_max[None], "blk", split_axis=1, concat_axis=0, tiled=True),
        lax.all_to_all(row_sum[None], "blk", split_axis=1, concat_axis=0, tiled=True),
        lax.all_to_all(row_out[None], "blk", split_axis=1, concat_axis=0, tiled=True),
    )
    global_max = jnp.max(peer_max, axis=0)
    factor = jnp.exp(peer_max - global_max[None])
    total_sum = jnp.sum(factor * peer_sum, axis=0)
    total_out = jnp.sum(factor[..., None] * peer_out, axis=0)
    return (total_out / total_sum[..., None]).astype(jnp.bfloat16)


def solution(mesh):
    in_specs = (
        P(("groups", "blk"), ("head", "sub"), None),
        P("head", ("groups", "blk"), None, None),
        P("head", ("groups", "blk"), None, None),
        P("groups"),
        P("groups"),
        P("groups"),
    )
    out_specs = P(("groups", "blk"), ("head", "sub"), None)
    return jax.shard_map(
        per_device, mesh=mesh, in_specs=in_specs, out_specs=out_specs, check_vma=False
    )
```

profile of v0, /device:TPU:0, one launch (start us, length us, event | category | flops | bytes accessed | tf_op | source)
XLA Modules:
  0.0 134.8 jit_solution(18213344517576960101)
XLA Ops:
  0.0 1.2 slice_bitcast_fusion.1
  1.2 4.1 %collective-permute-start = (bf16[8,256,128]{2,1,0:T(8,128)(2,1)S(1)}, bf16[8,256,128]{2,1,0:T(8,128)(2,1)S(1)}, u32[]{:S(2)}, u32[]{:S(2)}) collective-permute-start(bf16[8,256,128]{2,1,0:T(8,128)(2,1)S(1)} %slice_bitcast_fusion.1), channel_id=1, source_target_pairs={{0,8},{4,12},{8,0},{12,4},{1,9},{5,13},{9,1},{13,5},{2,10},{6,14},... | collective-permute-start | bytes 1572872 | tf_op jit(solution)/shard_map/ppermute | solution.py:10
  9.2 50.1 %all_gather.3 = bf16[64,8,128]{2,1,0:T(8,128)(2,1)S(1)} all-gather(bf16[16,8,128]{2,1,0:T(8,128)(2,1)S(1)} %copy-done.2), channel_id=1, replica_groups=mesh['groups'=2,'blk'=4,'head'=2,'sub'=2] {'blk'}, dimensions={0}, use_global_device_ids=true | all-gather | bytes 163840 | tf_op jit(solution)/shard_map/all_gather | solution.py:82
  61.4 41.1 %while.30 = (s32[]{:T(128)}, f32[512]{0:T(512)S(1)}, f32[512]{0:T(512)S(1)}, f32[512,128]{1,0:T(8,128)}, s32[]{:T(128)}, /*index=5*/s32[16]{0:T(128)S(1)}, bf16[...) while((s32[]{:T(128)}, f32[512]{0:T(512)S(1)}, ...), condition=%wide.region_3.4_spmd.clone, body=%wide.region_0.3_spmd.clone.sunk | while | flops 68814080 | bytes 2408907 | solution.py:44
  64.0 2.0 %convolution_add_fusion.4 = f32[512,128]{1,0:T(8,128)} fusion(f32[512,256]{0,1:T(8,128)S(1)} %get-tuple-element.344, f32[512,128]{1,0:T(8,128)} %get-tuple-element.378, f32[512]{0:T(512)S(1)} %max.18, s32[512]{0:T(512)S(1)} %lt.137, s32[256]{0:T(256)S(1)} %iota_add_fusion.4, f32[512]{0:T(512)S(1)} %get-tuple-element.346, ...), kind=kOutput, calls=%fused_computation.5.clone.1 | convolution fusion | flops 34209792 | bytes 1121284 | tf_op jit(solution)/shard_map/while/body/dot_general | solution.py:26
  67.3 1.1 fusion.54
  68.6 2.0 %convolution_add_fusion.4 = f32[512,128]{1,0:T(8,128)} fusion(f32[512,256]{0,1:T(8,128)S(1)} %get-tuple-element.344, f32[512,128]{1,0:T(8,128)} %get-tuple-element.378, f32[512]{0:T(512)S(1)} %max.18, s32[512]{0:T(512)S(1)} %lt.137, s32[256]{0:T(256)S(1)} %iota_add_fusion.4, f32[512]{0:T(512)S(1)} %get-tuple-element.346, ...), kind=kOutput, calls=%fused_computation.5.clone.1 | convolution fusion | flops 34209792 | bytes 1121284 | tf_op jit(solution)/shard_map/while/body/dot_general | solution.py:26
  71.8 1.1 fusion.54
  73.1 2.0 %convolution_add_fusion.4 = f32[512,128]{1,0:T(8,128)} fusion(f32[512,256]{0,1:T(8,128)S(1)} %get-tuple-element.344, f32[512,128]{1,0:T(8,128)} %get-tuple-element.378, f32[512]{0:T(512)S(1)} %max.18, s32[512]{0:T(512)S(1)} %lt.137, s32[256]{0:T(256)S(1)} %iota_add_fusion.4, f32[512]{0:T(512)S(1)} %get-tuple-element.346, ...), kind=kOutput, calls=%fused_computation.5.clone.1 | convolution fusion | flops 34209792 | bytes 1121284 | tf_op jit(solution)/shard_map/while/body/dot_general | solution.py:26
  76.4 1.1 fusion.54
  77.7 2.0 %convolution_add_fusion.4 = f32[512,128]{1,0:T(8,128)} fusion(f32[512,256]{0,1:T(8,128)S(1)} %get-tuple-element.344, f32[512,128]{1,0:T(8,128)} %get-tuple-element.378, f32[512]{0:T(512)S(1)} %max.18, s32[512]{0:T(512)S(1)} %lt.137, s32[256]{0:T(256)S(1)} %iota_add_fusion.4, f32[512]{0:T(512)S(1)} %get-tuple-element.346, ...), kind=kOutput, calls=%fused_computation.5.clone.1 | convolution fusion | flops 34209792 | bytes 1121284 | tf_op jit(solution)/shard_map/while/body/dot_general | solution.py:26
  81.0 1.1 fusion.54
  82.2 2.0 %convolution_add_fusion.4 = f32[512,128]{1,0:T(8,128)} fusion(f32[512,256]{0,1:T(8,128)S(1)} %get-tuple-element.344, f32[512,128]{1,0:T(8,128)} %get-tuple-element.378, f32[512]{0:T(512)S(1)} %max.18, s32[512]{0:T(512)S(1)} %lt.137, s32[256]{0:T(256)S(1)} %iota_add_fusion.4, f32[512]{0:T(512)S(1)} %get-tuple-element.346, ...), kind=kOutput, calls=%fused_computation.5.clone.1 | convolution fusion | flops 34209792 | bytes 1121284 | tf_op jit(solution)/shard_map/while/body/dot_general | solution.py:26
  85.5 1.1 fusion.54
  86.8 2.0 %convolution_add_fusion.4 = f32[512,128]{1,0:T(8,128)} fusion(f32[512,256]{0,1:T(8,128)S(1)} %get-tuple-element.344, f32[512,128]{1,0:T(8,128)} %get-tuple-element.378, f32[512]{0:T(512)S(1)} %max.18, s32[512]{0:T(512)S(1)} %lt.137, s32[256]{0:T(256)S(1)} %iota_add_fusion.4, f32[512]{0:T(512)S(1)} %get-tuple-element.346, ...), kind=kOutput, calls=%fused_computation.5.clone.1 | convolution fusion | flops 34209792 | bytes 1121284 | tf_op jit(solution)/shard_map/while/body/dot_general | solution.py:26
  90.1 1.1 fusion.54
  91.4 2.0 %convolution_add_fusion.4 = f32[512,128]{1,0:T(8,128)} fusion(f32[512,256]{0,1:T(8,128)S(1)} %get-tuple-element.344, f32[512,128]{1,0:T(8,128)} %get-tuple-element.378, f32[512]{0:T(512)S(1)} %max.18, s32[512]{0:T(512)S(1)} %lt.137, s32[256]{0:T(256)S(1)} %iota_add_fusion.4, f32[512]{0:T(512)S(1)} %get-tuple-element.346, ...), kind=kOutput, calls=%fused_computation.5.clone.1 | convolution fusion | flops 34209792 | bytes 1121284 | tf_op jit(solution)/shard_map/while/body/dot_general | solution.py:26
  95.9 2.0 %convolution_add_fusion.4 = f32[512,128]{1,0:T(8,128)} fusion(f32[512,256]{0,1:T(8,128)S(1)} %get-tuple-element.344, f32[512,128]{1,0:T(8,128)} %get-tuple-element.378, f32[512]{0:T(512)S(1)} %max.18, s32[512]{0:T(512)S(1)} %lt.137, s32[256]{0:T(256)S(1)} %iota_add_fusion.4, f32[512]{0:T(512)S(1)} %get-tuple-element.346, ...), kind=kOutput, calls=%fused_computation.5.clone.1 | convolution fusion | flops 34209792 | bytes 1121284 | tf_op jit(solution)/shard_map/while/body/dot_general | solution.py:26
  100.5 2.0 %convolution_add_fusion.4 = f32[512,128]{1,0:T(8,128)} fusion(f32[512,256]{0,1:T(8,128)S(1)} %get-tuple-element.344, f32[512,128]{1,0:T(8,128)} %get-tuple-element.378, f32[512]{0:T(512)S(1)} %max.18, s32[512]{0:T(512)S(1)} %lt.137, s32[256]{0:T(256)S(1)} %iota_add_fusion.4, f32[512]{0:T(512)S(1)} %get-tuple-element.346, ...), kind=kOutput, calls=%fused_computation.5.clone.1 | convolution fusion | flops 34209792 | bytes 1121284 | tf_op jit(solution)/shard_map/while/body/dot_general | solution.py:26
  107.2 3.2 %all-to-all-start = ((f32[4,1,128]{2,1,0:T(1,128)}), f32[4,1,128]{2,1,0:T(1,128)S(1)}, u32[]{:S(2)}, u32[]{:S(2)}) async-start(f32[4,1,128]{2,1,0:T(1,128)} %reshape.47), calls=%async_computation | async-start | bytes 4096 | tf_op jit(solution)/shard_map/all_to_all | solution.py:100
  111.3 4.6 %all-to-all-done = f32[4,1,128]{2,1,0:T(1,128)S(1)} async-done(((f32[4,1,128]{2,1,0:T(1,128)}), f32[4,1,128]{2,1,0:T(1,128)S(1)}, u32[]{:S(2)}, u32[]{:S(2)}) %all-to-all-start) | async-done | bytes 2080 | tf_op jit(solution)/shard_map/all_to_all | solution.py:100
  115.9 7.9 %all_to_all.36 = f32[4,1,128]{2,1,0:T(1,128)S(1)} all-to-all(f32[4,1,128]{2,1,0:T(1,128)S(1)} %reshape.49), channel_id=1, replica_groups=mesh['groups'=2,'blk'=4,'head'=2,'sub'=2] {'blk'}, dimensions={0} | all-to-all | bytes 4096 | tf_op jit(solution)/shard_map/all_to_all | solution.py:101
  123.8 3.4 %all-to-all-start.1 = ((f32[1,64,8,128]{3,2,0,1:T(8,128)}), f32[1,64,8,128]{3,2,0,1:T(8,128)S(1)}, u32[]{:S(2)}, u32[]{:S(2)}) async-start(f32[1,64,8,128]{3,2,0,1:T(8,128)} %bitcast.9), calls=%async_computation.1 | async-start | bytes 524288 | tf_op jit(solution)/shard_map/all_to_all | solution.py:102
  128.8 5.2 %all-to-all-done.1 = f32[1,64,8,128]{3,2,0,1:T(8,128)S(1)} async-done(((f32[1,64,8,128]{3,2,0,1:T(8,128)}), f32[1,64,8,128]{3,2,0,1:T(8,128)S(1)}, u32[]{:S(2)}, u32[]{:S(2)}) %all-to-all-start.1) | async-done | bytes 262176 | tf_op jit(solution)/shard_map/all_to_all | solution.py:102
  (111 shorter events, 20.0 us)
Async XLA Ops:
  0.0 5.3 %copy-start = (bf16[1,16,256,128]{3,2,1,0:T(8,128)(2,1)S(1)}, bf16[1,16,256,128]{3,2,1,0:T(8,128)(2,1)}, u32[]{:S(2)}) copy-start(bf16[1,16,256,128]{3,2,1,0:T(8,128)(2,1)} %param.12) | copy-start | bytes 3145732
  1.2 104.0 %collective-permute-start = (bf16[8,256,128]{2,1,0:T(8,128)(2,1)S(1)}, bf16[8,256,128]{2,1,0:T(8,128)(2,1)S(1)}, u32[]{:S(2)}, u32[]{:S(2)}) collective-permute-start(bf16[8,256,128]{2,1,0:T(8,128)(2,1)S(1)} %slice_bitcast_fusion.1), channel_id=1, source_target_pairs={{0,8},{4,12},{8,0},{12,4},{1,9},{5,13},{9,1},{13,5},{2,10},{6,14},... | collective-permute-start | bytes 1572872 | tf_op jit(solution)/shard_map/ppermute | solution.py:10
  5.3 0.7 copy-start.3
  5.3 99.8 %collective-permute-start.1 = (bf16[8,256,128]{2,1,0:T(8,128)(2,1)S(1)}, bf16[8,256,128]{2,1,0:T(8,128)(2,1)S(1)}, u32[]{:S(2)}, u32[]{:S(2)}) collective-permute-start(bf16[8,256,128]{2,1,0:T(8,128)(2,1)S(1)} %slice_bitcast_fusion), channel_id=1, source_target_pairs={{0,8},{4,12},{8,0},{12,4},{1,9},{5,13},{9,1},{13,5},{2,10},{6,14},... | collective-permute-start | bytes 1572872 | tf_op jit(solution)/shard_map/ppermute | solution.py:10
  5.6 3.6 %copy-start.2 = (bf16[16,8,128]{2,1,0:T(8,128)(2,1)S(1)}, bf16[16,8,128]{2,1,0:T(8,128)(2,1)}, u32[]{:S(2)}) copy-start(bf16[16,8,128]{2,1,0:T(8,128)(2,1)} %param.10) | copy-start | bytes 98308
  59.3 0.7 copy-start.4
  60.8 0.7 copy-start.1
  107.2 8.7 %all-to-all-start = ((f32[4,1,128]{2,1,0:T(1,128)}), f32[4,1,128]{2,1,0:T(1,128)S(1)}, u32[]{:S(2)}, u32[]{:S(2)}) async-start(f32[4,1,128]{2,1,0:T(1,128)} %reshape.47), calls=%async_computation | async-start | bytes 4096 | tf_op jit(solution)/shard_map/all_to_all | solution.py:100
  123.8 10.2 %all-to-all-start.1 = ((f32[1,64,8,128]{3,2,0,1:T(8,128)}), f32[1,64,8,128]{3,2,0,1:T(8,128)S(1)}, u32[]{:S(2)}, u32[]{:S(2)}) async-start(f32[1,64,8,128]{3,2,0,1:T(8,128)} %bitcast.9), calls=%async_computation.1 | async-start | bytes 524288 | tf_op jit(solution)/shard_map/all_to_all | solution.py:102
where the time goes:
time: 134 us; the launch traced here: 135 us
  blocking collectives  58 us (43%)
  matrix products  27.9 us (21%)
  local copies, waits for them, and re-layouts  12.6 us (9%)
  starting transfers between devices  11 us (8%)
  waiting for transfers between devices  9.76 us (7%)
  between operations  5.25 us (4%)
  loops' own time  5.21 us (4%)
  other arithmetic  5.04 us (4%)
    all_gather x1, blocking collectives, per_device(): all_queries = lax.all_gather(queries, 'blk', axis=0, tiled=True)  50.1 us
    dot_general x9, matrix products, block_update(): jnp.dot(weights.astype(jnp.bfloat16), value_block, preferred_element_type...  18.1 us
    dot_general x9, matrix products, block_update(): jnp.dot(q_rows, key_block.T, preferred_element_type=jnp.float32)  9.8 us
    all_to_all x1, blocking collectives, per_device(): lax.all_to_all(row_sum[None], 'blk', split_axis=1, concat_axis=0, tiled=T...  7.9 us
    another operation x2, loops' own time, run_slots(): return lax.fori_loop(lower_slot, upper_slot, loop_body, running)  5.21 us
    all_to_all x1, waiting for transfers between devices, per_device(): lax.all_to_all(row_out[None], 'blk', split_axis=1, concat_axis=0, tiled=T...  5.18 us
    dynamic_slice x9, local copies, waits for them, and re-layouts, loop_body(): slot_ids[slot_number]  4.96 us
    all_to_all x1, waiting for transfers between devices, per_device(): lax.all_to_all(row_max[None], 'blk', split_axis=1, concat_axis=0, tiled=T...  4.57 us
  transfers between devices with their start and end apart: 4, of which 2 were waited for; matrix products, arithmetic and copies ran while one was open for 30% of the time, Pallas kernels for 0%

commit v1 on v0

v1 whole, which is shorter than its diff:
```python
import functools

import jax
import jax.numpy as jnp
from jax import lax
from jax.experimental import pallas as pl
from jax.experimental.pallas import tpu as pltpu
from jax.sharding import PartitionSpec as P

masked_score = -1e30
lowest_max = -1e29
stat_rows = 16
tile_blocks = 2
log2_e = 1.4426950408889634


def split_three(x):
    high = x.astype(jnp.bfloat16)
    rest = x - high.astype(jnp.float32)
    middle = rest.astype(jnp.bfloat16)
    low = (rest - middle.astype(jnp.float32)).astype(jnp.bfloat16)
    return high, middle, low


def attend_kernel(
    sources, counts_ref, blocks_ref, offsets_ref, *refs
):
    n = len(sources)
    q_refs, (k_ref, v_ref), out_refs = refs[:n], refs[n : n + 2], refs[n + 2 : 2 * n + 2]
    score_ref, limit_ref, sum_ref = refs[2 * n + 2 :]
    rows, width = q_refs[0].shape
    slots, block_len, _ = k_ref.shape
    tokens = offsets_ref.shape[0] // lax.axis_size("blk")
    heads = rows // tokens
    member = lax.axis_index("blk")
    members = lax.axis_size("blk")
    count = counts_ref[member]
    tiles = (count + tile_blocks - 1) // tile_blocks
    scale = width ** (-0.5) * log2_e
    lanes = 128
    tile_len = tile_blocks * block_len

    least = offsets_ref[0] * 0 + 2**30
    for part, shift in enumerate(sources):
        home = lax.rem(member + members - shift, members)
        for t in range(tokens):
            limit = offsets_ref[home * tokens + t]
            least = jnp.minimum(least, limit)
            limit_ref[part, t * heads : (t + 1) * heads, :] = jnp.full((heads, lanes), limit, jnp.int32)

    def first_of(slot):
        live = slot < count
        index = blocks_ref[member * slots + slot]
        return jnp.where(live, index * block_len, 2**30)

    lane = lax.broadcasted_iota(jnp.int32, (rows, lanes), 1)

    def score_tile(tile, tops):
        slot = tile * tile_blocks
        firsts = [first_of(slot + i) for i in range(tile_blocks)]
        last = firsts[0]
        for first in firsts[1:]:
            last = jnp.maximum(last, first)

        def tile_scores(part, i):
            return lax.dot_general(
                q_refs[part][...],
                k_ref[slot + i],
                (((1,), (1,)), ((), ())),
                preferred_element_type=jnp.float32,
            )

        def plain(tops):
            out = []
            for part in range(n):
                top = tops[part]
                for i in range(tile_blocks):
                    s = tile_scores(part, i)
                    score_ref[part, tile, :, i * block_len : (i + 1) * block_len] = s
                    for c in range(0, block_len, lanes):
                        top = jnp.maximum(top, s[:, c : c + lanes])
                out.append(top)
            return tuple(out)

        def masking(tops):
            out = []
            for part in range(n):
                top = tops[part]
                for i in range(tile_blocks):
                    s = tile_scores(part, i)
                    for c in range(0, block_len, lanes):
                        seen = lane < limit_ref[part] - (firsts[i] + c)
                        piece = jnp.where(seen, s[:, c : c + lanes], masked_score)
                        at = i * block_len + c
                        score_ref[part, tile, :, at : at + lanes] = piece
                        top = jnp.maximum(top, piece)
                out.append(top)
            return tuple(out)

        return lax.cond(last + block_len <= least, plain, masking, tops)

    tops = tuple(jnp.full((rows, lanes), lowest_max, jnp.float32) for _ in range(n))
    tops = lax.fori_loop(0, tiles, score_tile, tops)
    tops = [jnp.max(top, axis=1, keepdims=True) * scale for top in tops]

    def value_tile(tile, carried):
        slot = tile * tile_blocks
        values = v_ref[pl.ds(slot, tile_blocks)].reshape(tile_len, width)
        out = []
        for part in range(n):
            total, summed = carried[part]
            weights = jnp.exp2(score_ref[part, tile] * scale - tops[part])
            for c in range(0, tile_len, lanes):
                total = total + weights[:, c : c + lanes]
            summed = summed + jnp.dot(
                weights.astype(jnp.bfloat16), values, preferred_element_type=jnp.float32
            )
            out.append((total, summed))
        return tuple(out)

    zero = jnp.zeros((rows, lanes), jnp.float32)
    zero_out = jnp.zeros((rows, width), jnp.float32)
    carried = lax.fori_loop(0, tiles, value_tile, tuple((zero, zero_out) for _ in range(n)))
    for part in range(n):
        total = jnp.sum(carried[part][0], axis=1, keepdims=True)
        empty = total <= 0.0
        safe = jnp.where(empty, 1.0, total)
        out_refs[part][:rows, :] = (carried[part][1] / safe).astype(jnp.bfloat16)
        level = jnp.where(empty, masked_score, tops[part] + jnp.log2(safe))
        levels = jnp.transpose(jnp.broadcast_to(level, (rows, lanes)))[:stat_rows]
        high, middle, low = split_three(levels)
        row = lax.broadcasted_iota(jnp.int32, levels.shape, 0)
        packed = jnp.where(
            row == 0,
            high.astype(jnp.float32),
            jnp.where(row == 1, middle.astype(jnp.float32), low.astype(jnp.float32)),
        )
        out_refs[part][rows:, :] = packed.astype(jnp.bfloat16)


def attend(sources, queries, keys, values, counts, blocks, offsets):
    n = len(sources)
    rows, width = queries[0].shape
    slots, block_len, _ = keys.shape
    tiles = slots // tile_blocks
    smem = pl.BlockSpec(memory_space=pltpu.SMEM)
    vmem = pl.BlockSpec(memory_space=pltpu.VMEM)
    return pl.pallas_call(
        functools.partial(attend_kernel, sources),
        out_shape=[jax.ShapeDtypeStruct((rows + stat_rows, width), jnp.bfloat16)] * n,
        in_specs=[smem] * 3 + [vmem] * (n + 2),
        out_specs=[vmem] * n,
        scratch_shapes=[
            pltpu.VMEM((n, tiles, rows, tile_blocks * block_len), jnp.float32),
            pltpu.VMEM((n, rows, 128), jnp.int32),
            pltpu.VMEM((8, 128), jnp.float32),
        ],
        cost_estimate=pl.CostEstimate(
            flops=4 * n * rows * width * slots * block_len,
            bytes_accessed=4 * slots * block_len * width,
            transcendentals=n * rows * slots * block_len,
        ),
        name=f"attend_{n}",
    )(counts, blocks, offsets, *queries, keys, values)


def merge_kernel(*refs):
    parts, out_ref = refs[:-1], refs[-1]
    rows, width = out_ref.shape
    levels = []
    for part in parts:
        stats = part[rows:, :].astype(jnp.float32)
        levels.append(stats[0:1] + stats[1:2] + stats[2:3])
    top = functools.reduce(jnp.maximum, levels)
    weights = [jnp.exp2(level - top) for level in levels]
    total = functools.reduce(lambda a, b: a + b, weights)
    summed = jnp.zeros((rows, width), jnp.float32)
    for part, weight in zip(parts, weights):
        column = jnp.transpose(jnp.broadcast_to(weight / total, (width, rows)))
        summed = summed + column * part[:rows, :].astype(jnp.float32)
    out_ref[...] = summed.astype(jnp.bfloat16)


def merge(parts, rows, width):
    vmem = pl.BlockSpec(memory_space=pltpu.VMEM)
    return pl.pallas_call(
        merge_kernel,
        out_shape=jax.ShapeDtypeStruct((rows, width), jnp.bfloat16),
        in_specs=[vmem] * len(parts),
        out_specs=vmem,
        name="merge",
    )(*parts)


def shifted(x, shift):
    members = lax.axis_size("blk")
    return lax.ppermute(x, "blk", [(i, (i + shift) % members) for i in range(members)])


def per_device(queries, key_cache, cached_value_slots, block_counts, slot_blocks, offsets):
    tokens, heads, width = queries.shape
    members = lax.axis_size("blk")
    own = queries.reshape(tokens * heads, width)
    held = [own] + [shifted(own, s) for s in range(1, members)]
    parts = attend(
        tuple(range(members)),
        held,
        key_cache[0],
        cached_value_slots[0],
        block_counts,
        slot_blocks,
        offsets,
    )
    back = [parts[0]] + [shifted(parts[s], -s) for s in range(1, members)]
    return merge(back, tokens * heads, width).reshape(tokens, heads, width)


def solution(mesh):
    in_specs = (
        P(("groups", "blk"), ("head", "sub"), None),
        P("head", ("groups", "blk"), None, None),
        P("head", ("groups", "blk"), None, None),
        P("groups"),
        P("groups"),
        P("groups"),
    )
    out_specs = P(("groups", "blk"), ("head", "sub"), None)
    return jax.shard_map(
        per_device, mesh=mesh, in_specs=in_specs, out_specs=out_specs, check_vma=False
    )
```

time: 134 us -> 29.5 us (0.22)
  blocking collectives: 58 us -> 0 us
  matrix products: 27.9 us -> 0 us
  local copies, waits for them, and re-layouts: 12.6 us -> 1.23 us
  Pallas kernels: 0 us -> 10.3 us
  between operations: 5.25 us -> 0.02 us
  loops' own time: 5.21 us -> 0 us
  other arithmetic: 5.04 us -> 0 us
  starting transfers between devices: 11 us -> 8.11 us
    all_gather x1 -> x0, blocking collectives: 50.1 us -> none  [per_device(): all_queries = lax.all_gather(queries, 'blk', axis=0, tiled=True)]
    dot_general x18 -> x0, matrix products: 27.9 us -> none  [the longest x9 18.1 us: block_update(): jnp.dot(weights.astype(jnp.bfloat16), value_block, preferred_element_type...]
    pallas_call x0 -> x2, Pallas kernels: none -> 10.3 us  [the longest x1 8.71 us: attend(): pl.pallas_call(functools.partial(attend_kernel, sources), out_shape=[jax....]
    ppermute x2 -> x6, waiting for transfers between devices: 0.01 us -> 9.8 us  [shifted(): lax.ppermute(x, 'blk', [(i, (i + shift) % members) for i in range(members)])]
    all_to_all x2 -> x0, waiting for transfers between devices: 9.76 us -> none  [the longest x1 5.18 us: per_device(): lax.all_to_all(row_out[None], 'blk', split_axis=1, concat_axis=0, tiled=T...]
    all_to_all x1 -> x0, blocking collectives: 7.9 us -> none  [per_device(): lax.all_to_all(row_sum[None], 'blk', split_axis=1, concat_axis=0, tiled=T...]
    all_to_all x2 -> x0, starting transfers between devices: 6.63 us -> none  [the longest x1 3.4 us: per_device(): lax.all_to_all(row_out[None], 'blk', split_axis=1, concat_axis=0, tiled=T...]
    dynamic_slice x12 -> x0, local copies, waits for them, and re-layouts: 5.76 us -> none  [the longest x9 4.96 us: loop_body(): slot_ids[slot_number]]
  transfers between devices with their start and end apart: 4 -> 6, of which waited for: 2 -> 6; matrix products, arithmetic and copies ran while one was open for 30% -> 0% of each run, Pallas kernels for 0% -> 0%
where the time goes in v1:
time: 29.5 us
  Pallas kernels  10.3 us (35%)
  waiting for transfers between devices  9.8 us (33%)
  starting transfers between devices  8.11 us (27%)
  local copies, waits for them, and re-layouts  1.23 us (4%)
    ppermute x6, waiting for transfers between devices, shifted(): lax.ppermute(x, 'blk', [(i, (i + shift) % members) for i in range(members)])  9.8 us
    pallas_call x1, Pallas kernels, attend(): pl.pallas_call(functools.partial(attend_kernel, sources), out_shape=[jax....  8.71 us
    ppermute x6, starting transfers between devices, shifted(): lax.ppermute(x, 'blk', [(i, (i + shift) % members) for i in range(members)])  8.11 us
    pallas_call x1, Pallas kernels, merge(): pl.pallas_call(merge_kernel, out_shape=jax.ShapeDtypeStruct((rows, width)...  1.6 us
    unnamed x12, local copies, waits for them, and re-layouts  1.23 us
  transfers between devices with their start and end apart: 6, of which 6 were waited for; matrix products, arithmetic and copies ran while one was open for 0% of the time, Pallas kernels for 0%

profile of v1, /device:TPU:0, one launch (start us, length us, event | category | flops | bytes accessed | tf_op | source)
XLA Modules:
  0.0 29.5 jit_solution(11986515245562715981)
XLA Ops:
  0.0 5.1 %collective-permute-start.2 = (bf16[128,128]{1,0:T(8,128)(2,1)}, bf16[128,128]{1,0:T(8,128)(2,1)S(1)}, u32[]{:S(2)}, u32[]{:S(2)}) collective-permute-start(bf16[128,128]{1,0:T(8,128)(2,1)} %bitcast.6), channel_id=1, source_target_pairs={{0,12},{4,0},{8,4},{12,8},{1,13},{5,1},{9,5},{13,9},{2,14},{6,2},{... | collective-permute-start | bytes 98312 | tf_op jit(solution)/shard_map/ppermute | solution.py:197
  5.1 0.0 collective-permute-start.1
  5.1 1.0 %collective-permute-start = (bf16[128,128]{1,0:T(8,128)(2,1)}, bf16[128,128]{1,0:T(8,128)(2,1)S(1)}, u32[]{:S(2)}, u32[]{:S(2)}) collective-permute-start(bf16[128,128]{1,0:T(8,128)(2,1)} %bitcast.8), channel_id=1, source_target_pairs={{0,4},{4,8},{8,12},{12,0},{1,5},{5,9},{9,13},{13,1},{2,6},{6,10},{... | collective-permute-start | bytes 98312 | tf_op jit(solution)/shard_map/ppermute | solution.py:197
  6.1 0.9 %collective-permute-done.2.refs_3_ = bf16[128,128]{1,0:T(8,128)(2,1)S(1)} collective-permute-done((bf16[128,128]{1,0:T(8,128)(2,1)}, bf16[128,128]{1,0:T(8,128)(2,1)S(1)}, u32[]{:S(2)}, u32[]{:S(2)}) %collective-permute-start.2) | collective-permute-done | bytes 32800 | tf_op jit(solution)/shard_map/ppermute | solution.py:197
  7.0 0.0 copy-start.3
  7.0 3.1 %collective-permute-done.1.refs_2_ = bf16[128,128]{1,0:T(8,128)(2,1)S(1)} collective-permute-done((bf16[128,128]{1,0:T(8,128)(2,1)}, bf16[128,128]{1,0:T(8,128)(2,1)S(1)}, u32[]{:S(2)}, u32[]{:S(2)}) %collective-permute-start.1) | collective-permute-done | bytes 32800 | tf_op jit(solution)/shard_map/ppermute | solution.py:197
  10.1 0.0 copy-start.4
  10.1 0.9 %collective-permute-done.refs_1_ = bf16[128,128]{1,0:T(8,128)(2,1)S(1)} collective-permute-done((bf16[128,128]{1,0:T(8,128)(2,1)}, bf16[128,128]{1,0:T(8,128)(2,1)S(1)}, u32[]{:S(2)}, u32[]{:S(2)}) %collective-permute-start) | collective-permute-done | bytes 32800 | tf_op jit(solution)/shard_map/ppermute | solution.py:197
  11.0 0.0 copy-start.5
  11.0 0.0 copy-done.3
  11.0 0.0 copy-done.4
  11.0 0.6 %copy-done.5 = bf16[128,128]{1,0:T(8,128)(2,1)} copy-done((bf16[128,128]{1,0:T(8,128)(2,1)}, bf16[128,128]{1,0:T(8,128)(2,1)S(1)}, u32[]{:S(2)}) %copy-start.5) | copy-done | bytes 32792
  11.6 8.7 %attend_4.1 = (bf16[144,128]{1,0:T(8,128)(2,1)}, bf16[144,128]{1,0:T(8,128)(2,1)}, bf16[144,128]{1,0:T(8,128)(2,1)}, bf16[144,128]{1,0:T(8,128)(2,1)}) custom-call(s32[4]{0:T(128)} %counts_ref.1, s32[64]{0:T(128)} %blocks_ref.1, s32[64]{0:T(128)} %offsets_ref.1, bf16[128,128]{1,0:T(8,128)(2,1)} %bitcast.9, bf16[128,128]{1,0:T(8,128)(2,1)} %copy-done.5, ...), custom_call_target="tpu_custom_call" | custom-call | flops 1073741824 | bytes 2097152 | tf_op jit(solution)/shard_map/attend_4/pallas_call | solution.py:148
  20.3 0.0 collective-permute-start.3
  20.3 0.1 collective-permute-start.4
  20.4 1.9 %collective-permute-start.5 = (bf16[144,128]{1,0:T(8,128)(2,1)}, bf16[144,128]{1,0:T(8,128)(2,1)S(1)}, u32[]{:S(2)}, u32[]{:S(2)}) collective-permute-start(bf16[144,128]{1,0:T(8,128)(2,1)} %get-tuple-element.12), channel_id=1, source_target_pairs={{0,4},{4,8},{8,12},{12,0},{1,5},{5,9},{9,13},{13,1},{2,6},{6,10},{... | collective-permute-start | bytes 110600 | tf_op jit(solution)/shard_map/ppermute | solution.py:197
  22.4 2.4 %collective-permute-done.3.refs_1_ = bf16[144,128]{1,0:T(8,128)(2,1)S(1)} collective-permute-done((bf16[144,128]{1,0:T(8,128)(2,1)}, bf16[144,128]{1,0:T(8,128)(2,1)S(1)}, u32[]{:S(2)}, u32[]{:S(2)}) %collective-permute-start.3) | collective-permute-done | bytes 36896 | tf_op jit(solution)/shard_map/ppermute | solution.py:197
  24.8 0.0 copy-start
  24.8 0.7 %collective-permute-done.4.refs_2_ = bf16[144,128]{1,0:T(8,128)(2,1)S(1)} collective-permute-done((bf16[144,128]{1,0:T(8,128)(2,1)}, bf16[144,128]{1,0:T(8,128)(2,1)S(1)}, u32[]{:S(2)}, u32[]{:S(2)}) %collective-permute-start.4) | collective-permute-done | bytes 36896 | tf_op jit(solution)/shard_map/ppermute | solution.py:197
  25.5 1.8 %collective-permute-done.5.refs_3_ = bf16[144,128]{1,0:T(8,128)(2,1)S(1)} collective-permute-done((bf16[144,128]{1,0:T(8,128)(2,1)}, bf16[144,128]{1,0:T(8,128)(2,1)S(1)}, u32[]{:S(2)}, u32[]{:S(2)}) %collective-permute-start.5) | collective-permute-done | bytes 36896 | tf_op jit(solution)/shard_map/ppermute | solution.py:197
  27.3 0.0 copy-done
  27.3 0.0 copy-done.1
  27.3 0.6 %copy-done.2 = bf16[144,128]{1,0:T(8,128)(2,1)} copy-done((bf16[144,128]{1,0:T(8,128)(2,1)}, bf16[144,128]{1,0:T(8,128)(2,1)S(1)}, u32[]{:S(2)}) %copy-start.2) | copy-done | bytes 36888
  27.9 1.6 %merge.1 = bf16[128,128]{1,0:T(8,128)(2,1)} custom-call(bf16[144,128]{1,0:T(8,128)(2,1)} %get-tuple-element.9.refs_0_, bf16[144,128]{1,0:T(8,128)(2,1)} %copy-done, bf16[144,128]{1,0:T(8,128)(2,1)} %copy-done.1, bf16[144,128]{1,0:T(8,128)(2,1)} %copy-done.2), custom_call_target="tpu_custom_call" | custom-call | tf_op jit(solution)/shard_map/merge/pallas_call | solution.py:186
  (2 shorter events, 0.0 us)
Async XLA Ops:
  0.0 7.0 %collective-permute-start.2 = (bf16[128,128]{1,0:T(8,128)(2,1)}, bf16[128,128]{1,0:T(8,128)(2,1)S(1)}, u32[]{:S(2)}, u32[]{:S(2)}) collective-permute-start(bf16[128,128]{1,0:T(8,128)(2,1)} %bitcast.6), channel_id=1, source_target_pairs={{0,12},{4,0},{8,4},{12,8},{1,13},{5,1},{9,5},{13,9},{2,14},{6,2},{... | collective-permute-start | bytes 98312 | tf_op jit(solution)/shard_map/ppermute | solution.py:197
  5.1 5.0 %collective-permute-start.1 = (bf16[128,128]{1,0:T(8,128)(2,1)}, bf16[128,128]{1,0:T(8,128)(2,1)S(1)}, u32[]{:S(2)}, u32[]{:S(2)}) collective-permute-start(bf16[128,128]{1,0:T(8,128)(2,1)} %bitcast.7), channel_id=1, source_target_pairs={{0,8},{4,12},{8,0},{12,4},{1,9},{5,13},{9,1},{13,5},{2,10},{6,14},... | collective-permute-start | bytes 98312 | tf_op jit(solution)/shard_map/ppermute | solution.py:197
  5.1 5.9 %collective-permute-start = (bf16[128,128]{1,0:T(8,128)(2,1)}, bf16[128,128]{1,0:T(8,128)(2,1)S(1)}, u32[]{:S(2)}, u32[]{:S(2)}) collective-permute-start(bf16[128,128]{1,0:T(8,128)(2,1)} %bitcast.8), channel_id=1, source_target_pairs={{0,4},{4,8},{8,12},{12,0},{1,5},{5,9},{9,13},{13,1},{2,6},{6,10},{... | collective-permute-start | bytes 98312 | tf_op jit(solution)/shard_map/ppermute | solution.py:197
  7.0 4.0 %copy-start.3 = (bf16[128,128]{1,0:T(8,128)(2,1)}, bf16[128,128]{1,0:T(8,128)(2,1)S(1)}, u32[]{:S(2)}) copy-start(bf16[128,128]{1,0:T(8,128)(2,1)S(1)} %collective-permute-done.2.refs_3_) | copy-start | bytes 98308
  10.1 0.9 %copy-start.4 = (bf16[128,128]{1,0:T(8,128)(2,1)}, bf16[128,128]{1,0:T(8,128)(2,1)S(1)}, u32[]{:S(2)}) copy-start(bf16[128,128]{1,0:T(8,128)(2,1)S(1)} %collective-permute-done.1.refs_2_) | copy-start | bytes 98308
  11.0 0.6 %copy-start.5 = (bf16[128,128]{1,0:T(8,128)(2,1)}, bf16[128,128]{1,0:T(8,128)(2,1)S(1)}, u32[]{:S(2)}) copy-start(bf16[128,128]{1,0:T(8,128)(2,1)S(1)} %collective-permute-done.refs_1_) | copy-start | bytes 98308
  20.3 4.5 %collective-permute-start.3 = (bf16[144,128]{1,0:T(8,128)(2,1)}, bf16[144,128]{1,0:T(8,128)(2,1)S(1)}, u32[]{:S(2)}, u32[]{:S(2)}) collective-permute-start(bf16[144,128]{1,0:T(8,128)(2,1)} %get-tuple-element.10), channel_id=1, source_target_pairs={{0,12},{4,0},{8,4},{12,8},{1,13},{5,1},{9,5},{13,9},{2,14},{6,2},{... | collective-permute-start | bytes 110600 | tf_op jit(solution)/shard_map/ppermute | solution.py:197
  20.3 5.1 %collective-permute-start.4 = (bf16[144,128]{1,0:T(8,128)(2,1)}, bf16[144,128]{1,0:T(8,128)(2,1)S(1)}, u32[]{:S(2)}, u32[]{:S(2)}) collective-permute-start(bf16[144,128]{1,0:T(8,128)(2,1)} %get-tuple-element.11), channel_id=1, source_target_pairs={{0,8},{4,12},{8,0},{12,4},{1,9},{5,13},{9,1},{13,5},{2,10},{6,14},... | collective-permute-start | bytes 110600 | tf_op jit(solution)/shard_map/ppermute | solution.py:197
  20.4 6.8 %collective-permute-start.5 = (bf16[144,128]{1,0:T(8,128)(2,1)}, bf16[144,128]{1,0:T(8,128)(2,1)S(1)}, u32[]{:S(2)}, u32[]{:S(2)}) collective-permute-start(bf16[144,128]{1,0:T(8,128)(2,1)} %get-tuple-element.12), channel_id=1, source_target_pairs={{0,4},{4,8},{8,12},{12,0},{1,5},{5,9},{9,13},{13,1},{2,6},{6,10},{... | collective-permute-start | bytes 110600 | tf_op jit(solution)/shard_map/ppermute | solution.py:197
  24.8 2.5 %copy-start = (bf16[144,128]{1,0:T(8,128)(2,1)}, bf16[144,128]{1,0:T(8,128)(2,1)S(1)}, u32[]{:S(2)}) copy-start(bf16[144,128]{1,0:T(8,128)(2,1)S(1)} %collective-permute-done.3.refs_1_) | copy-start | bytes 110596
  25.5 1.8 %copy-start.1 = (bf16[144,128]{1,0:T(8,128)(2,1)}, bf16[144,128]{1,0:T(8,128)(2,1)S(1)}, u32[]{:S(2)}) copy-start(bf16[144,128]{1,0:T(8,128)(2,1)S(1)} %collective-permute-done.4.refs_2_) | copy-start | bytes 110596
  27.3 0.6 %copy-start.2 = (bf16[144,128]{1,0:T(8,128)(2,1)}, bf16[144,128]{1,0:T(8,128)(2,1)S(1)}, u32[]{:S(2)}) copy-start(bf16[144,128]{1,0:T(8,128)(2,1)S(1)} %collective-permute-done.5.refs_3_) | copy-start | bytes 110596

commit v2 on v1

v2 whole, which is shorter than its diff:
```python
import functools

import jax
import jax.numpy as jnp
from jax import lax
from jax.experimental import pallas as pl
from jax.experimental.pallas import tpu as pltpu
from jax.sharding import PartitionSpec as P

masked_score = -1e30
lowest_max = -1e29
lanes = 128
stat_rows = 16
tile_blocks = 4
log2_e = 1.4426950408889634
far = 2**30


def split_three(x):
    high = x.astype(jnp.bfloat16)
    rest = x - high.astype(jnp.float32)
    middle = rest.astype(jnp.bfloat16)
    low = (rest - middle.astype(jnp.float32)).astype(jnp.bfloat16)
    return high.astype(jnp.float32), middle.astype(jnp.float32), low.astype(jnp.float32)


def attend_rows(
    home, counts_ref, blocks_ref, offsets_ref, q_ref, k_ref, v_ref, part_ref, score_ref, room_ref, ready
):
    rows, width = q_ref.shape
    slots, block_len, _ = k_ref.shape
    members = lax.axis_size("blk")
    member = lax.axis_index("blk")
    tokens = offsets_ref.shape[0] // members
    heads = rows // tokens
    count = counts_ref[member]
    tiles = (count + tile_blocks - 1) // tile_blocks
    scale = width ** (-0.5) * log2_e
    tile_len = tile_blocks * block_len

    lane = lax.broadcasted_iota(jnp.int32, (heads, lanes), 1)
    for t in range(tokens):
        room_ref[t * heads : (t + 1) * heads, :] = offsets_ref[home * tokens + t] - lane

    def score_tile(tile, top):
        ready(tile)
        for i in range(tile_blocks):
            slot = tile * tile_blocks + i
            first = jnp.where(slot < count, blocks_ref[member * slots + slot] * block_len, far)
            s = lax.dot_general(
                q_ref[...], k_ref[slot], (((1,), (1,)), ((), ())), preferred_element_type=jnp.float32
            )
            for c in range(0, block_len, lanes):
                piece = jnp.where(room_ref[...] > first + c, s[:, c : c + lanes], masked_score)
                at = i * block_len + c
                score_ref[tile, :, at : at + lanes] = piece
                top = jnp.maximum(top, piece)
        return top

    top = lax.fori_loop(0, tiles, score_tile, jnp.full((rows, lanes), lowest_max, jnp.float32))
    top = jnp.max(top, axis=1, keepdims=True) * scale

    def value_tile(tile, carried):
        total, summed = carried
        values = v_ref[pl.ds(tile * tile_blocks, tile_blocks)].reshape(tile_len, width)
        weights = jnp.exp2(score_ref[tile] * scale - top)
        for c in range(0, tile_len, lanes):
            total = total + weights[:, c : c + lanes]
        summed = summed + jnp.dot(
            weights.astype(jnp.bfloat16), values, preferred_element_type=jnp.float32
        )
        return total, summed

    zero = (jnp.zeros((rows, lanes), jnp.float32), jnp.zeros((rows, width), jnp.float32))
    total, summed = lax.fori_loop(0, tiles, value_tile, zero)
    total = jnp.sum(total, axis=1, keepdims=True)
    empty = total <= 0.0
    safe = jnp.where(empty, 1.0, total)
    part_ref[:rows, :] = (summed / safe).astype(jnp.bfloat16)
    level = jnp.where(empty, masked_score, top + jnp.log2(safe))
    levels = jnp.transpose(jnp.broadcast_to(level, (rows, lanes)))[:stat_rows]
    high, middle, low = split_three(levels)
    row = lax.broadcasted_iota(jnp.int32, levels.shape, 0)
    packed = jnp.where(row == 0, high, jnp.where(row == 1, middle, low))
    part_ref[rows:, :] = packed.astype(jnp.bfloat16)


def first_kernel(
    counts_ref, blocks_ref, offsets_ref, q_ref, k_hbm, v_hbm,
    part_ref, k_ref, v_ref, score_ref, room_ref, sems,
):
    member = lax.axis_index("blk")
    slots = k_ref.shape[0]
    tiles = (counts_ref[member] + tile_blocks - 1) // tile_blocks

    def copies(tile):
        here = pl.ds(tile * tile_blocks, tile_blocks)
        return (
            pltpu.make_async_copy(k_hbm.at[here], k_ref.at[here], sems.at[0, tile]),
            pltpu.make_async_copy(v_hbm.at[here], v_ref.at[here], sems.at[1, tile]),
        )

    for kind in range(2):
        for tile in range(slots // tile_blocks):

            @pl.when(tile < tiles)
            def _():
                copies(tile)[kind].start()

    def ready(tile):
        for copy in copies(tile):
            copy.wait()

    attend_rows(
        member, counts_ref, blocks_ref, offsets_ref, q_ref, k_ref, v_ref, part_ref,
        score_ref, room_ref, ready,
    )


def next_kernel(
    bit, counts_ref, blocks_ref, offsets_ref, q_ref, k_ref, v_ref, part_ref, score_ref, room_ref
):
    home = jnp.bitwise_xor(lax.axis_index("blk"), bit)
    attend_rows(
        home, counts_ref, blocks_ref, offsets_ref, q_ref, k_ref, v_ref, part_ref,
        score_ref, room_ref, lambda tile: None,
    )


def attend(bit, queries, keys, values, tables):
    rows, width = queries.shape
    slots, block_len, _ = keys.shape
    tiles = slots // tile_blocks
    smem = pl.BlockSpec(memory_space=pltpu.SMEM)
    vmem = pl.BlockSpec(memory_space=pltpu.VMEM)
    hbm = pl.BlockSpec(memory_space=pltpu.HBM)
    part = jax.ShapeDtypeStruct((rows + stat_rows, width), jnp.bfloat16)
    scratch = [
        pltpu.VMEM((tiles, rows, tile_blocks * block_len), jnp.float32),
        pltpu.VMEM((rows, lanes), jnp.int32),
    ]
    common = dict(
        cost_estimate=pl.CostEstimate(
            flops=4 * rows * width * slots * block_len,
            bytes_accessed=4 * slots * block_len * width,
            transcendentals=rows * slots * block_len,
        ),
        compiler_params=pltpu.CompilerParams(
            vmem_limit_bytes=4 * rows * slots * block_len + 8 * slots * block_len * width + 2**21
        ),
        name=f"attend_{bit}",
    )
    if bit == 0:
        return pl.pallas_call(
            first_kernel,
            out_shape=[part, keys, values],
            in_specs=[smem] * 3 + [vmem, hbm, hbm],
            out_specs=[vmem] * 3,
            scratch_shapes=scratch + [pltpu.SemaphoreType.DMA((2, tiles))],
            **common,
        )(*tables, queries, keys, values)
    return pl.pallas_call(
        functools.partial(next_kernel, bit),
        out_shape=part,
        in_specs=[smem] * 3 + [vmem] * 3,
        out_specs=vmem,
        scratch_shapes=scratch,
        **common,
    )(*tables, queries, keys, values)


def merge_kernel(*refs):
    parts, out_ref = refs[:-1], refs[-1]
    rows, width = out_ref.shape
    levels = []
    for part in parts:
        stats = part[rows:, :].astype(jnp.float32)
        levels.append(stats[0:1] + stats[1:2] + stats[2:3])
    top = functools.reduce(jnp.maximum, levels)
    weights = [jnp.exp2(level - top) for level in levels]
    total = functools.reduce(lambda a, b: a + b, weights)
    summed = jnp.zeros((rows, width), jnp.float32)
    for part, weight in zip(parts, weights):
        column = jnp.transpose(jnp.broadcast_to(weight / total, (width, rows)))
        summed = summed + column * part[:rows, :].astype(jnp.float32)
    out_ref[...] = summed.astype(jnp.bfloat16)


def merge(parts, rows, width):
    vmem = pl.BlockSpec(memory_space=pltpu.VMEM)
    return pl.pallas_call(
        merge_kernel,
        out_shape=jax.ShapeDtypeStruct((rows, width), jnp.bfloat16),
        in_specs=[vmem] * len(parts),
        out_specs=vmem,
        compiler_params=pltpu.CompilerParams(vmem_limit_bytes=2**21),
        name="merge",
    )(*parts)


def swapped(x, bit):
    return lax.ppermute(x, "blk", [(i, i ^ bit) for i in range(lax.axis_size("blk"))])


def per_device(queries, key_cache, cached_value_slots, block_counts, slot_blocks, offsets):
    tokens, heads, width = queries.shape
    members = lax.axis_size("blk")
    own = queries.reshape(tokens * heads, width)
    tables = (block_counts, slot_blocks, offsets)
    held = {bit: swapped(own, bit) for bit in range(1, members)}
    part, keys, values = attend(0, own, key_cache[0], cached_value_slots[0], tables)
    parts = [part]
    for bit in range(1, members):
        parts.append(swapped(attend(bit, held[bit], keys, values, tables), bit))
    return merge(parts, tokens * heads, width).reshape(tokens, heads, width)


def solution(mesh):
    in_specs = (
        P(("groups", "blk"), ("head", "sub"), None),
        P("head", ("groups", "blk"), None, None),
        P("head", ("groups", "blk"), None, None),
        P("groups"),
        P("groups"),
        P("groups"),
    )
    out_specs = P(("groups", "blk"), ("head", "sub"), None)
    return jax.shard_map(
        per_device, mesh=mesh, in_specs=in_specs, out_specs=out_specs, check_vma=False
    )
```

time: 29.5 us -> 28 us (0.949); the launches traced: 29.5 us -> 27.5 us
  waiting for transfers between devices: 9.8 us -> 2.94 us
  starting transfers between devices: 8.11 us -> 12.5 us
  local copies, waits for them, and re-layouts: 1.23 us -> 3.89 us
  Pallas kernels: 10.3 us -> 8.21 us
    ppermute x6, waiting for transfers between devices: 9.8 us -> 2.94 us  [swapped(): lax.ppermute(x, 'blk', [(i, i ^ bit) for i in range(lax.axis_size('blk'))])]
    ppermute x6, starting transfers between devices: 8.11 us -> 12.5 us  [swapped(): lax.ppermute(x, 'blk', [(i, i ^ bit) for i in range(lax.axis_size('blk'))])]
    unnamed x12, local copies, waits for them, and re-layouts: 1.23 us -> 3.89 us
    pallas_call x1 -> x4, Pallas kernels: 8.71 us -> 7.43 us  [the longest x3 5.42 us: attend(): pl.pallas_call(functools.partial(next_kernel, bit), out_shape=part, in_sp...]
    pallas_call x1, Pallas kernels: 1.6 us -> 0.78 us  [merge(): pl.pallas_call(merge_kernel, out_shape=jax.ShapeDtypeStruct((rows, width)...]
  transfers between devices with their start and end apart: 6 -> 6, of which waited for: 6 -> 2; matrix products, arithmetic and copies ran while one was open for 0% -> 0% of each run, Pallas kernels for 0% -> 27%
where the time goes in v2:
time: 28 us; the launch traced here: 27.5 us
  starting transfers between devices  12.5 us (45%)
  Pallas kernels  8.21 us (29%)
  local copies, waits for them, and re-layouts  3.89 us (14%)
  waiting for transfers between devices  2.94 us (10%)
    ppermute x6, starting transfers between devices, swapped(): lax.ppermute(x, 'blk', [(i, i ^ bit) for i in range(lax.axis_size('blk'))])  12.5 us
    pallas_call x3, Pallas kernels, attend(): pl.pallas_call(functools.partial(next_kernel, bit), out_shape=part, in_sp...  5.42 us
    unnamed x12, local copies, waits for them, and re-layouts  3.89 us
    ppermute x6, waiting for transfers between devices, swapped(): lax.ppermute(x, 'blk', [(i, i ^ bit) for i in range(lax.axis_size('blk'))])  2.94 us
    pallas_call x1, Pallas kernels, attend(): pl.pallas_call(first_kernel, out_shape=[part, keys, values], in_specs=[sm...  2.01 us
    pallas_call x1, Pallas kernels, merge(): pl.pallas_call(merge_kernel, out_shape=jax.ShapeDtypeStruct((rows, width)...  0.78 us
  transfers between devices with their start and end apart: 6, of which 2 were waited for; matrix products, arithmetic and copies ran while one was open for 0% of the time, Pallas kernels for 27%

profile of v2, /device:TPU:0, one launch (start us, length us, event | category | flops | bytes accessed | tf_op | source)
XLA Modules:
  0.0 27.5 jit_solution(13638734438452555360)
XLA Ops:
  0.0 3.1 %collective-permute-start = (bf16[128,128]{1,0:T(8,128)(2,1)}, bf16[128,128]{1,0:T(8,128)(2,1)S(1)}, u32[]{:S(2)}, u32[]{:S(2)}) collective-permute-start(bf16[128,128]{1,0:T(8,128)(2,1)} %bitcast.6), channel_id=1, source_target_pairs={{0,4},{4,0},{8,12},{12,8},{1,5},{5,1},{9,13},{13,9},{2,6},{6,2},{1... | collective-permute-start | bytes 98312 | tf_op jit(solution)/shard_map/ppermute | solution.py:202
  3.1 2.5 %collective-permute-start.4 = (bf16[128,128]{1,0:T(8,128)(2,1)}, bf16[128,128]{1,0:T(8,128)(2,1)S(1)}, u32[]{:S(2)}, u32[]{:S(2)}) collective-permute-start(bf16[128,128]{1,0:T(8,128)(2,1)} %bitcast.7), channel_id=1, source_target_pairs={{0,12},{4,8},{8,4},{12,0},{1,13},{5,9},{9,5},{13,1},{2,14},{6,10},... | collective-permute-start | bytes 98312 | tf_op jit(solution)/shard_map/ppermute | solution.py:202
  5.5 0.1 collective-permute-start.2
  5.6 0.0 copy-start.3
  5.7 0.6 %copy-done.3 = s32[4]{0:T(128)S(1)} copy-done((s32[4]{0:T(128)S(1)}, s32[4]{0:T(128)}, u32[]{:S(2)}) %copy-start.3) | copy-done | bytes 40
  6.3 0.0 copy-done.4
  6.3 0.0 copy-done.5
  6.3 1.2 %copy-done = bf16[1,16,256,128]{3,2,1,0:T(8,128)(2,1)S(1)} copy-done((bf16[1,16,256,128]{3,2,1,0:T(8,128)(2,1)S(1)}, bf16[1,16,256,128]{3,2,1,0:T(8,128)(2,1)}, u32[]{:S(2)}) %copy-start) | copy-done | bytes 1048600
  7.6 1.2 %copy-done.1 = bf16[1,16,256,128]{3,2,1,0:T(8,128)(2,1)S(1)} copy-done((bf16[1,16,256,128]{3,2,1,0:T(8,128)(2,1)S(1)}, bf16[1,16,256,128]{3,2,1,0:T(8,128)(2,1)}, u32[]{:S(2)}) %copy-start.1) | copy-done | bytes 1048600
  8.8 0.8 %copy-done.2 = bf16[16,8,128]{2,1,0:T(8,128)(2,1)S(1)} copy-done((bf16[16,8,128]{2,1,0:T(8,128)(2,1)S(1)}, bf16[16,8,128]{2,1,0:T(8,128)(2,1)}, u32[]{:S(2)}) %copy-start.2) | copy-done | bytes 32792
  9.5 2.0 %attend_0.1 = (bf16[144,128]{1,0:T(8,128)(2,1)S(1)}, bf16[16,256,128]{2,1,0:T(8,128)(2,1)S(1)}, bf16[16,256,128]{2,1,0:T(8,128)(2,1)S(1)}) custom-call(s32[4]{0:T(128)S(1)} %copy-done.3, s32[64]{0:T(128)S(1)} %copy-done.4, s32[64]{0:T(128)S(1)} %copy-done.5, bf16[128,128]{1,0:T(8,128)(2,1)S(1)} %bitcast.9, bf16[16,256,128]{2,1,0:T(8,128)(2,1)S(1)} %bitcast.4, ...), custom_call_target="tpu_custom_call" | custom-call | flops 268435456 | bytes 2097152 | tf_op jit(solution)/shard_map/attend_0/pallas_call | solution.py:154
  11.6 0.0 collective-permute-done.q_ref
  11.6 1.8 %attend_1.1 = bf16[144,128]{1,0:T(8,128)(2,1)S(1)} custom-call(s32[4]{0:T(128)S(1)} %copy-done.3, s32[64]{0:T(128)S(1)} %copy-done.4, s32[64]{0:T(128)S(1)} %copy-done.5, bf16[128,128]{1,0:T(8,128)(2,1)S(1)} %collective-permute-done.q_ref, bf16[16,256,128]{2,1,0:T(8,128)(2,1)S(1)} %get-tuple-element.9.k_ref, bf16[16,256,128]{2,1,0:T(8,128)(2,1)S(1)} %get-tuple-element.10.v_ref), custom_call_target="tpu_custom_call" | custom-call | flops 268435456 | bytes 2097152 | tf_op jit(solution)/shard_map/attend_1/pallas_call | solution.py:162
  13.4 3.9 %collective-permute-start.1 = (bf16[144,128]{1,0:T(8,128)(2,1)S(1)}, bf16[144,128]{1,0:T(8,128)(2,1)S(1)}, u32[]{:S(2)}, u32[]{:S(2)}) collective-permute-start(bf16[144,128]{1,0:T(8,128)(2,1)S(1)} %attend_1.1), channel_id=1, source_target_pairs={{0,4},{4,0},{8,12},{12,8},{1,5},{5,1},{9,13},{13,9},{2,6},{6,2},{1... | collective-permute-start | bytes 110600 | tf_op jit(solution)/shard_map/ppermute | solution.py:202
  17.3 0.0 collective-permute-done.2.q_ref
  17.3 1.8 %attend_2.1 = bf16[144,128]{1,0:T(8,128)(2,1)S(1)} custom-call(s32[4]{0:T(128)S(1)} %copy-done.3, s32[64]{0:T(128)S(1)} %copy-done.4, s32[64]{0:T(128)S(1)} %copy-done.5, bf16[128,128]{1,0:T(8,128)(2,1)S(1)} %collective-permute-done.2.q_ref, bf16[16,256,128]{2,1,0:T(8,128)(2,1)S(1)} %get-tuple-element.9.k_ref, bf16[16,256,128]{2,1,0:T(8,128)(2,1)S(1)} %get-tuple-element.10.v_ref), custom_call_target="tpu_custom_call" | custom-call | flops 268435456 | bytes 2097152 | tf_op jit(solution)/shard_map/attend_2/pallas_call | solution.py:162
  19.1 0.0 collective-permute-start.3
  19.1 0.0 collective-permute-done.4.q_ref
  19.1 1.8 %attend_3.1 = bf16[144,128]{1,0:T(8,128)(2,1)S(1)} custom-call(s32[4]{0:T(128)S(1)} %copy-done.3, s32[64]{0:T(128)S(1)} %copy-done.4, s32[64]{0:T(128)S(1)} %copy-done.5, bf16[128,128]{1,0:T(8,128)(2,1)S(1)} %collective-permute-done.4.q_ref, bf16[16,256,128]{2,1,0:T(8,128)(2,1)S(1)} %get-tuple-element.9.k_ref, bf16[16,256,128]{2,1,0:T(8,128)(2,1)S(1)} %get-tuple-element.10.v_ref), custom_call_target="tpu_custom_call" | custom-call | flops 268435456 | bytes 2097152 | tf_op jit(solution)/shard_map/attend_3/pallas_call | solution.py:162
  20.9 2.9 %collective-permute-start.5 = (bf16[144,128]{1,0:T(8,128)(2,1)S(1)}, bf16[144,128]{1,0:T(8,128)(2,1)S(1)}, u32[]{:S(2)}, u32[]{:S(2)}) collective-permute-start(bf16[144,128]{1,0:T(8,128)(2,1)S(1)} %attend_3.1), channel_id=1, source_target_pairs={{0,12},{4,8},{8,4},{12,0},{1,13},{5,9},{9,5},{13,1},{2,14},{6,10},... | collective-permute-start | bytes 110600 | tf_op jit(solution)/shard_map/ppermute | solution.py:202
  23.8 0.0 collective-permute-done.1.refs_1_
  23.8 0.1 collective-permute-done.3.refs_2_
  24.0 2.8 %collective-permute-done.5.refs_3_ = bf16[144,128]{1,0:T(8,128)(2,1)S(1)} collective-permute-done((bf16[144,128]{1,0:T(8,128)(2,1)S(1)}, bf16[144,128]{1,0:T(8,128)(2,1)S(1)}, u32[]{:S(2)}, u32[]{:S(2)}) %collective-permute-start.5) | collective-permute-done | bytes 36896 | tf_op jit(solution)/shard_map/ppermute | solution.py:202
  26.8 0.8 %merge.1 = bf16[128,128]{1,0:T(8,128)(2,1)} custom-call(bf16[144,128]{1,0:T(8,128)(2,1)S(1)} %get-tuple-element.8.refs_0_, bf16[144,128]{1,0:T(8,128)(2,1)S(1)} %collective-permute-done.1.refs_1_, bf16[144,128]{1,0:T(8,128)(2,1)S(1)} %collective-permute-done.3.refs_2_, bf16[144,128]{1,0:T(8,128)(2,1)S(1)} %collective-permute-done.5.refs_3_), custom_call_target="tpu_custom_call" | custom-call | tf_op jit(solution)/shard_map/merge/pallas_call | solution.py:191
  (5 shorter events, 0.0 us)
Async XLA Ops:
  0.0 11.6 %collective-permute-start = (bf16[128,128]{1,0:T(8,128)(2,1)}, bf16[128,128]{1,0:T(8,128)(2,1)S(1)}, u32[]{:S(2)}, u32[]{:S(2)}) collective-permute-start(bf16[128,128]{1,0:T(8,128)(2,1)} %bitcast.6), channel_id=1, source_target_pairs={{0,4},{4,0},{8,12},{12,8},{1,5},{5,1},{9,13},{13,9},{2,6},{6,2},{1... | collective-permute-start | bytes 98312 | tf_op jit(solution)/shard_map/ppermute | solution.py:202
  3.1 16.1 %collective-permute-start.4 = (bf16[128,128]{1,0:T(8,128)(2,1)}, bf16[128,128]{1,0:T(8,128)(2,1)S(1)}, u32[]{:S(2)}, u32[]{:S(2)}) collective-permute-start(bf16[128,128]{1,0:T(8,128)(2,1)} %bitcast.7), channel_id=1, source_target_pairs={{0,12},{4,8},{8,4},{12,0},{1,13},{5,9},{9,5},{13,1},{2,14},{6,10},... | collective-permute-start | bytes 98312 | tf_op jit(solution)/shard_map/ppermute | solution.py:202
  5.5 11.7 %collective-permute-start.2 = (bf16[128,128]{1,0:T(8,128)(2,1)}, bf16[128,128]{1,0:T(8,128)(2,1)S(1)}, u32[]{:S(2)}, u32[]{:S(2)}) collective-permute-start(bf16[128,128]{1,0:T(8,128)(2,1)} %bitcast.8), channel_id=1, source_target_pairs={{0,8},{4,12},{8,0},{12,4},{1,9},{5,13},{9,1},{13,5},{2,10},{6,14},... | collective-permute-start | bytes 98312 | tf_op jit(solution)/shard_map/ppermute | solution.py:202
  5.6 0.7 %copy-start.3 = (s32[4]{0:T(128)S(1)}, s32[4]{0:T(128)}, u32[]{:S(2)}) copy-start(s32[4]{0:T(128)} %counts_ref.7) | copy-start | bytes 52
  5.6 0.7 %copy-start.4 = (s32[64]{0:T(128)S(1)}, s32[64]{0:T(128)}, u32[]{:S(2)}) copy-start(s32[64]{0:T(128)} %blocks_ref.7) | copy-start | bytes 772
  5.7 0.7 %copy-start.5 = (s32[64]{0:T(128)S(1)}, s32[64]{0:T(128)}, u32[]{:S(2)}) copy-start(s32[64]{0:T(128)} %offsets_ref.7) | copy-start | bytes 772
  6.3 1.2 %copy-start = (bf16[1,16,256,128]{3,2,1,0:T(8,128)(2,1)S(1)}, bf16[1,16,256,128]{3,2,1,0:T(8,128)(2,1)}, u32[]{:S(2)}) copy-start(bf16[1,16,256,128]{3,2,1,0:T(8,128)(2,1)} %param.7) | copy-start | bytes 3145732
  7.6 1.2 %copy-start.1 = (bf16[1,16,256,128]{3,2,1,0:T(8,128)(2,1)S(1)}, bf16[1,16,256,128]{3,2,1,0:T(8,128)(2,1)}, u32[]{:S(2)}) copy-start(bf16[1,16,256,128]{3,2,1,0:T(8,128)(2,1)} %param.8) | copy-start | bytes 3145732
  8.8 0.8 %copy-start.2 = (bf16[16,8,128]{2,1,0:T(8,128)(2,1)S(1)}, bf16[16,8,128]{2,1,0:T(8,128)(2,1)}, u32[]{:S(2)}) copy-start(bf16[16,8,128]{2,1,0:T(8,128)(2,1)} %param.6) | copy-start | bytes 98308
  13.4 10.5 %collective-permute-start.1 = (bf16[144,128]{1,0:T(8,128)(2,1)S(1)}, bf16[144,128]{1,0:T(8,128)(2,1)S(1)}, u32[]{:S(2)}, u32[]{:S(2)}) collective-permute-start(bf16[144,128]{1,0:T(8,128)(2,1)S(1)} %attend_1.1), channel_id=1, source_target_pairs={{0,4},{4,0},{8,12},{12,8},{1,5},{5,1},{9,13},{13,9},{2,6},{6,2},{1... | collective-permute-start | bytes 110600 | tf_op jit(solution)/shard_map/ppermute | solution.py:202
  19.1 4.9 %collective-permute-start.3 = (bf16[144,128]{1,0:T(8,128)(2,1)S(1)}, bf16[144,128]{1,0:T(8,128)(2,1)S(1)}, u32[]{:S(2)}, u32[]{:S(2)}) collective-permute-start(bf16[144,128]{1,0:T(8,128)(2,1)S(1)} %attend_2.1), channel_id=1, source_target_pairs={{0,8},{4,12},{8,0},{12,4},{1,9},{5,13},{9,1},{13,5},{2,10},{6,14},... | collective-permute-start | bytes 110600 | tf_op jit(solution)/shard_map/ppermute | solution.py:202
  20.9 5.8 %collective-permute-start.5 = (bf16[144,128]{1,0:T(8,128)(2,1)S(1)}, bf16[144,128]{1,0:T(8,128)(2,1)S(1)}, u32[]{:S(2)}, u32[]{:S(2)}) collective-permute-start(bf16[144,128]{1,0:T(8,128)(2,1)S(1)} %attend_3.1), channel_id=1, source_target_pairs={{0,12},{4,8},{8,4},{12,0},{1,13},{5,9},{9,5},{13,1},{2,14},{6,10},... | collective-permute-start | bytes 110600 | tf_op jit(solution)/shard_map/ppermute | solution.py:202
